TPU v7x, 256 devices: a whole 4x4x8 slice. The times are simulated.
256 devices in a mesh: blk: 64 (over x, y_hi, z), con: 4 (over y_lo, core).
Axes of the slice: x: 4, y: 4 (y_hi: 2, y_lo: 2; y = y_hi * 2 + y_lo), z: 8, core: 2. Of those that a mesh axis runs over, the one named last changes fastest.
Arguments:
- patch_rows: bfloat16 [4, 12288, 16, 1024], P('con', 'blk'), may hold values from -6 to 6
- subject_ids: int32 [12288], replicated, may hold values from 0 to 3071
- logit_scale: float32 [2], replicated, may hold values from 5 to 20
- logit_bias: float32 [2], replicated, may hold values from -6 to -2
Outputs:
- grad_emb: float32 [4, 12288, 1024], P('con', 'blk')
All inputs are finite; a program needn't handle non-finite values.
Results may differ from a plain program's by a relative error of at most 0.0037.
Values may be sent and summed in bfloat16 or wider, within the bound.
No kernel may reach another device: no remote copies, remote signals or barrier semaphores. Data moves between devices by JAX's collectives and lax.ppermute only.
A program may use at most 128 MiB of HBM per device.

v0:
```python
import jax
import jax.numpy as jnp
from jax import lax
from jax.sharding import PartitionSpec as P


def from_partner(shard, axis, stride):
    return lax.ppermute(shard, axis, [(i, i ^ 1 << stride) for i in range(lax.axis_size(axis))])


def on_device(patch_rows, subject_ids, logit_scale, logit_bias):
    row_count = patch_rows.shape[1]
    patch_count = patch_rows.shape[2]
    width = patch_rows.shape[3]
    pooled = jnp.sum(patch_rows[0], axis=1, dtype=jnp.float32) / patch_count
    row_norms = jnp.sqrt(jnp.sum(pooled * pooled, axis=1, keepdims=True) + 1e-06)
    own_emb = (pooled / row_norms).astype(jnp.bfloat16)
    contrast = lax.axis_index("con")
    pair_index = contrast // 2
    scale_value = logit_scale[pair_index]
    bias_value = logit_bias[pair_index]
    position = lax.axis_index("blk")
    own_ids = lax.dynamic_slice_in_dim(subject_ids, position * row_count, row_count, 0)
    partner = from_partner(own_emb, "con", 0)
    shard_rows = lax.all_gather(partner, "blk", axis=0, tiled=True)
    logits = (
        scale_value
        * lax.dot_general(
            own_emb, shard_rows, (((1,), (1,)), ((), ())), preferred_element_type=jnp.float32
        )
        + bias_value
    )
    label_sign = jnp.where(own_ids[:, None] == subject_ids[None, :], 1.0, -1.0).astype(jnp.float32)
    coeff = (scale_value * (jax.nn.sigmoid(label_sign * logits) - 1.0) * label_sign).astype(
        jnp.bfloat16
    )
    gradient = jnp.dot(coeff, shard_rows, preferred_element_type=jnp.float32)
    return gradient.reshape(1, row_count, width)


def solution(mesh):
    in_specs = (P("con", "blk", None, None), P(), P(), P())
    out_specs = P("con", "blk", None)
    return jax.shard_map(
        on_device, mesh=mesh, in_specs=in_specs, out_specs=out_specs, check_vma=False
    )
```

profile of v0, /device:TPU:1, one launch (start us, length us, event | category | flops | bytes accessed | tf_op | source)
XLA Modules:
  0.0 312.9 jit_solution(6936567670982369488)
XLA Ops:
  6.5 0.0 copy-start.2
  6.5 0.0 copy-start.3
  6.5 0.0 copy-start.1
  6.5 0.0 all-gather.2.cloned.1.call-start
  6.5 6.1 %convert_reduce_fusion = f32[192,1024]{1,0:T(8,128)S(1)} fusion(bf16[1,192,16,1024]{3,2,1,0:T(8,128)(2,1)} %param.4), kind=kLoop, calls=%fused_computation.11 | loop fusion | flops 6094848 | bytes 7077888 | tf_op jit(solution)/shard_map/reduce_sum | solution.py:15
  12.6 0.2 multiply_reduce_fusion
  12.8 0.1 divide_convert_fusion
  12.9 3.3 %collective-permute-start = (bf16[192,1024]{1,0:T(8,128)(2,1)S(1)}, bf16[192,1024]{1,0:T(8,128)(2,1)S(1)}, u32[]{:S(2)}, u32[]{:S(2)}) collective-permute-start(bf16[192,1024]{1,0:T(8,128)(2,1)S(1)} %divide_convert_fusion), channel_id=1, source_target_pairs={{0,1},{1,0},{2,3},{3,2},{4,5},{5,4},{6,7},{7,6},{8,9},{9,8},{10,11... | collective-permute-start | bytes 1179656 | tf_op jit(solution)/shard_map/ppermute | solution.py:8
  16.2 1.3 collective-permute-done
  17.6 0.0 copy-start
  17.6 0.7 copy-done
  18.3 0.0 all-gather.2.cloned.1.call-update
  18.4 0.0 copy-done.2
  18.4 0.6 dynamic_slice.11
  19.0 0.0 copy-done.3
  19.0 0.6 dynamic_slice.9
  19.6 0.0 copy-done.1
  19.6 0.1 dynamic_slice.10
  19.7 258.4 %all-gather.2.cloned.1.call-done = bf16[12288,1024]{1,0:T(8,128)(2,1)} async-done(((bf16[192,1024]{1,0:T(8,128)(2,1)}), bf16[12288,1024]{1,0:T(8,128)(2,1)}) %all-gather.2.cloned.1.call-update) | async-done | bytes 25165840 | tf_op jit(solution)/shard_map/all_gather | solution.py:25
  278.2 27.9 %fusion.17 = f32[1,192,1024]{2,1,0:T(8,128)} fusion(bf16[12288,1024]{1,0:T(8,128)(2,1)} %all-gather.2.cloned.1.call-done, bf16[192,1024]{1,0:T(8,128)(2,1)S(1)} %divide_convert_fusion, f32[]{:T(128)} %bitcast.1, s32[12288]{0:T(1024)S(1)} %copy-done.1, f32[]{:T(128)} %bitcast, s32[192]{0:T(256)S(1)} %dynamic_slice.10), kind=kOutput, calls=%fused_computation.19 | convolution fusion | flops 9691987968 | bytes 26395400 | tf_op jit(solution)/shard_map/dot_general | solution.py:37
  (1 shorter events, 0.0 us)
Async XLA Ops:
  6.5 11.8 %copy-start.2 = (f32[2]{0:T(128)S(1)}, f32[2]{0:T(128)}, u32[]{:S(2)}) copy-start(f32[2]{0:T(128)} %param.7) | copy-start | bytes 28
  6.5 12.4 %copy-start.3 = (f32[2]{0:T(128)S(1)}, f32[2]{0:T(128)}, u32[]{:S(2)}) copy-start(f32[2]{0:T(128)} %param.6) | copy-start | bytes 28
  6.5 13.1 %copy-start.1 = (s32[12288]{0:T(1024)S(1)}, s32[12288]{0:T(1024)}, u32[]{:S(2)}) copy-start(s32[12288]{0:T(1024)} %param.5) | copy-start | bytes 147460
  6.5 271.6 %all-gather.2.cloned.1.call-start = ((), (), s32[]{:S(2)}) async-start(), calls=%async_computation | async-start | bytes 25559040 | tf_op jit(solution)/shard_map/all_gather | solution.py:25
  12.9 4.6 %collective-permute-start = (bf16[192,1024]{1,0:T(8,128)(2,1)S(1)}, bf16[192,1024]{1,0:T(8,128)(2,1)S(1)}, u32[]{:S(2)}, u32[]{:S(2)}) collective-permute-start(bf16[192,1024]{1,0:T(8,128)(2,1)S(1)} %divide_convert_fusion), channel_id=1, source_target_pairs={{0,1},{1,0},{2,3},{3,2},{4,5},{5,4},{6,7},{7,6},{8,9},{9,8},{10,11... | collective-permute-start | bytes 1179656 | tf_op jit(solution)/shard_map/ppermute | solution.py:8
  17.6 0.7 copy-start
Sparse Core Ops, SparseCore 0:
  18.5 259.6 all-gather.1
where the time goes:
time: 313 us
  waiting for transfers between devices  260 us (83%)
  matrix products  27.9 us (9%)
  between operations  13.4 us (4%)
  other arithmetic  6.38 us (2%)
  starting transfers between devices  3.29 us (1%)
    all_gather x1, waiting for transfers between devices, on_device(): shard_rows = lax.all_gather(partner, 'blk', axis=0, tiled=True)  258 us
    dot_general x1, matrix products, on_device(): gradient = jnp.dot(coeff, shard_rows, preferred_element_type=jnp.float32)  27.9 us
  transfers between devices with their start and end apart: 2, of which 2 were waited for; matrix products, arithmetic and copies ran while one was open for 0% of the time, Pallas kernels for 0%

commit v1 on v0

--- a/solution.py
+++ b/solution.py
@@ -22,7 +22,8 @@
     position = lax.axis_index("blk")
     own_ids = lax.dynamic_slice_in_dim(subject_ids, position * row_count, row_count, 0)
     partner = from_partner(own_emb, "con", 0)
-    shard_rows = lax.all_gather(partner, "blk", axis=0, tiled=True)
+    sent = jnp.stack([partner] * lax.axis_size("blk"))
+    shard_rows = jnp.concatenate(lax.all_to_all(sent, "blk", 0, 0), axis=0)
     logits = (
         scale_value
         * lax.dot_general(

time: 313 us -> 680 us (2.17)
  the two profiles are of different devices: /device:TPU:1 before, /device:TPU:146 now
where the time goes in v1:
time: 680 us
  waiting for transfers between devices  622 us (91%)
  matrix products  28 us (4%)
  starting transfers between devices  13.1 us (2%)
  local copies, waits for them, and re-layouts  10 us (1%)
    all_to_all x1, waiting for transfers between devices, on_device(): shard_rows = jnp.concatenate(lax.all_to_all(sent, 'blk', 0, 0), axis=0)  620 us
    dot_general x1, matrix products, on_device(): gradient = jnp.dot(coeff, shard_rows, preferred_element_type=jnp.float32)  28 us
  transfers between devices with their start and end apart: 2, of which 2 were waited for; matrix products, arithmetic and copies ran while one was open for 0% of the time, Pallas kernels for 0%

profile of v1, /device:TPU:146, one launch (start us, length us, event | category | flops | bytes accessed | tf_op | source)
XLA Modules:
  0.0 679.6 jit_solution(5524196334629865819)
XLA Ops:
  0.0 6.1 convert_reduce_fusion
  6.1 0.2 multiply_reduce_fusion
  6.2 0.1 divide_convert_fusion
  6.4 0.1 collective-permute-start
  6.5 1.7 collective-permute-done
  8.2 8.6 %stack.2 = bf16[64,192,1024]{2,1,0:T(8,128)(2,1)} broadcast(bf16[192,1024]{1,0:T(8,128)(2,1)S(1)} %collective-permute-done), dimensions={1,2} | broadcast | bytes 25559040 | tf_op jit(solution)/shard_map/stack | solution.py:25
  16.8 0.0 copy-start.1
  16.9 0.0 copy-start.2
  16.9 0.0 copy-start
  16.9 13.0 %all-to-all-start = ((bf16[64,192,1024]{2,1,0:T(8,128)(2,1)}), bf16[64,192,1024]{2,1,0:T(8,128)(2,1)}, u32[]{:S(2)}, u32[]{:S(2)}) async-start(bf16[64,192,1024]{2,1,0:T(8,128)(2,1)} %stack.2), calls=%async_computation | async-start | bytes 50331648 | tf_op jit(solution)/shard_map/all_to_all | solution.py:26
  29.9 0.0 copy-done.1
  29.9 0.7 dynamic_slice.11
  30.5 0.0 copy-done.2
  30.5 0.6 dynamic_slice.9
  31.2 0.0 copy-done
  31.2 0.1 dynamic_slice.10
  31.2 620.4 %all-to-all-done = bf16[64,192,1024]{2,1,0:T(8,128)(2,1)} async-done(((bf16[64,192,1024]{2,1,0:T(8,128)(2,1)}), bf16[64,192,1024]{2,1,0:T(8,128)(2,1)}, u32[]{:S(2)}, u32[]{:S(2)}) %all-to-all-start) | async-done | bytes 25165856 | tf_op jit(solution)/shard_map/all_to_all | solution.py:26
  651.6 28.0 %fusion.17 = f32[1,192,1024]{2,1,0:T(8,128)} fusion(bf16[12288,1024]{1,0:T(8,128)(2,1)} %bitcast.1, bf16[192,1024]{1,0:T(8,128)(2,1)S(1)} %divide_convert_fusion, f32[]{:T(128)} %bitcast.2, s32[12288]{0:T(1024)S(1)} %copy-done, f32[]{:T(128)} %bitcast, s32[192]{0:T(256)S(1)} %dynamic_slice.10), kind=kOutput, calls=%fused_computation.19 | convolution fusion | flops 9691987968 | bytes 26395400 | tf_op jit(solution)/shard_map/dot_general | solution.py:38
  (1 shorter events, 0.0 us)
Async XLA Ops:
  6.4 1.8 collective-permute-start
  16.8 13.0 %copy-start.1 = (f32[2]{0:T(128)S(1)}, f32[2]{0:T(128)}, u32[]{:S(2)}) copy-start(f32[2]{0:T(128)} %param.7) | copy-start | bytes 28
  16.9 13.7 %copy-start.2 = (f32[2]{0:T(128)S(1)}, f32[2]{0:T(128)}, u32[]{:S(2)}) copy-start(f32[2]{0:T(128)} %param.6) | copy-start | bytes 28
  16.9 14.3 %copy-start = (s32[12288]{0:T(1024)S(1)}, s32[12288]{0:T(1024)}, u32[]{:S(2)}) copy-start(s32[12288]{0:T(1024)} %param.5) | copy-start | bytes 147460
  16.9 634.8 %all-to-all-start = ((bf16[64,192,1024]{2,1,0:T(8,128)(2,1)}), bf16[64,192,1024]{2,1,0:T(8,128)(2,1)}, u32[]{:S(2)}, u32[]{:S(2)}) async-start(bf16[64,192,1024]{2,1,0:T(8,128)(2,1)} %stack.2), calls=%async_computation | async-start | bytes 50331648 | tf_op jit(solution)/shard_map/all_to_all | solution.py:26
